TPU v7x, 128 devices: a whole 4x4x4 slice. The times are simulated.
128 devices in a mesh: seq: 32 (over x, z, core), tp: 4 (over y).
Axes of the slice: x: 4, y: 4, z: 4, core: 2. Of those that a mesh axis runs over, the one named last changes fastest.
Arguments:
- hidden: bfloat16 [384, 1024], P('seq'), may hold values from -60 to 60
- norm_gains: float32 [3, 1024], replicated, may hold values from 0.5 to 1.5
- w_qkv: bfloat16 [3, 1024, 1024], P(None, None, 'tp'), may hold values from -0.1875 to 0.1875
- w_self_out: bfloat16 [1024, 1024], P('tp'), may hold values from -0.1875 to 0.1875
- w_cross_q: bfloat16 [1024, 1024], P(None, 'tp'), may hold values from -0.1875 to 0.1875
- w_cross_out: bfloat16 [1024, 1024], P('tp'), may hold values from -0.1875 to 0.1875
- w_up: bfloat16 [1024, 8192], P(None, 'tp'), may hold values from -0.1875 to 0.1875
- w_down: bfloat16 [8192, 1024], P('tp'), may hold values from -0.0625 to 0.0625
- kv_cache: bfloat16 [2, 3072, 128, 1024], P(None, 'seq', None, 'tp'), may hold values from -70 to 70
- encoder_kv: bfloat16 [2, 96, 256, 1024], P(None, 'seq', None, 'tp'), may hold values from -70 to 70
- cache_lengths: int32 [96], replicated, may hold values from 129 to 65536, as said below
- page_table: int32 [96, 512], replicated, may hold values from -1 to 3071, as said below
- group_of: int32 [96], replicated, may hold values from 0 to 11, as said below
Outputs:
- updated: bfloat16 [384, 1024], P('seq', 'tp')
Inputs may be any that keep to these rules, and one draw needn't show every extreme that they name: `group_of`: each of the 12 groups holds exactly 8 requests. Request r has ceil(cache_lengths[r] / 128) pages in page_table, every one full but its last; some request has exactly 65536 positions. `page_table`: entry [r, j] is the global slot (device index along seq times 96 plus local slot) of request r's page j, or -1 past its last page. The requests of one group begin with the same full pages (their prompt); their other pages are their own. No slot serves two groups. On every device the used slots are its first ones, and some device uses all 96.
All inputs are finite; a program needn't handle non-finite values.
Results may differ from a plain program's by a relative error of at most 0.005.
The roundings to bfloat16 on the way count: a program that leaves them out, or rounds other values in their place, can miss the bound.
Values may be sent and summed in bfloat16 or wider, within the bound.
A program may use at most 128 MiB of HBM per device.

v0:
```python
import jax
import jax.numpy as jnp
from jax import lax
from jax.sharding import PartitionSpec as P

HD = 64
PAGE = 128
NEW = 4
GSIZE = 8


NEG_BIG = -1e30


def joined(shard, axis, combine):
    everything = jax.tree.map(lambda part: lax.all_gather(part, axis), shard)
    first = jax.tree.map(lambda part: part[0], everything)

    def step(k, so_far):
        return combine(so_far, jax.tree.map(lambda part: part[k], everything))

    return lax.fori_loop(1, lax.axis_size(axis), step, first)


def layer_norm(values, norm_gain):
    centre = values - jnp.mean(values, axis=-1, keepdims=True)
    spread = jnp.mean(centre * centre, axis=-1, keepdims=True)
    return centre * lax.rsqrt(spread + 1e-05) * norm_gain


def page_meta(page_table, group_of, cache_lengths, first_slot, slot_count, page_len, group_size):
    request_count, most_pages = page_table.shape
    flat_table = page_table.reshape(-1)
    logical = jnp.tile(jnp.arange(most_pages, dtype=jnp.int32), request_count)
    owner_ids = jnp.repeat(jnp.arange(request_count, dtype=jnp.int32), most_pages)
    local_slot = flat_table - first_slot
    inside = (flat_table >= 0) & (local_slot >= 0) & (local_slot < slot_count)
    target = jnp.where(inside, local_slot, slot_count)
    slot_page = jnp.zeros((slot_count + 1,), jnp.int32).at[target].max(logical)[:slot_count]
    slot_group = (
        jnp.zeros((slot_count + 1,), jnp.int32).at[target].max(group_of[owner_ids])[:slot_count]
    )
    in_use = (
        jnp.zeros((slot_count + 1,), jnp.int32).at[target].max(jnp.ones_like(target))[:slot_count]
    )
    members = jnp.argsort(group_of, stable=True).reshape(request_count // group_size, group_size)
    slot_members = members[slot_group]
    global_page = first_slot + jnp.arange(slot_count, dtype=jnp.int32)
    owned_page = page_table[slot_members, slot_page[:, None]] == global_page[:, None]
    position = slot_page[:, None] * page_len + jnp.arange(page_len, dtype=jnp.int32)[None, :]
    valid_keys = owned_page[:, :, None] & (
        position[:, None, :] < cache_lengths[slot_members][:, :, None]
    )
    return (slot_members, valid_keys, jnp.sum(in_use))


def fold_parts(running, peak_score, weight_sum, weighted, row_index, head_count):
    old_peak, old_sum, old_acc = running
    new_peak = old_peak.at[row_index].max(peak_score)
    keep_factor = jnp.exp(old_peak - new_peak)
    factor = jnp.exp(peak_score - new_peak[row_index])
    new_sum = (old_sum * keep_factor).at[row_index].add(weight_sum * factor)
    head_width = old_acc.shape[1] // head_count
    scaled_acc = old_acc.reshape(-1, head_count, head_width) * keep_factor[:, :, None]
    new_acc = (
        scaled_acc.at[row_index]
        .add(weighted * factor[:, :, None])
        .reshape(-1, head_count * head_width)
    )
    return (new_peak, new_sum, new_acc)


def page_block(running, page_keys, page_values, query_heads, slot_members, valid_keys):
    new_count = query_heads.shape[1]
    head_count = query_heads.shape[2]
    picked = query_heads[slot_members]
    scores = jnp.einsum(
        "sgthe,skhe->sgthk", picked, page_keys, preferred_element_type=jnp.float32
    ) * HD ** (-0.5)
    key_mask = valid_keys[:, :, None, None, :]
    scores = jnp.where(key_mask, scores, NEG_BIG)
    peak_score = jnp.max(scores, axis=-1)
    exponent = jnp.where(key_mask, jnp.exp(scores - peak_score[..., None]), 0.0)
    weight_sum = jnp.sum(exponent, axis=-1)
    rounded = exponent.astype(jnp.bfloat16)
    weighted = jnp.einsum(
        "sgthk,skhe->sgthe", rounded, page_values, preferred_element_type=jnp.float32
    )
    row_index = (
        slot_members[:, :, None] * new_count + jnp.arange(new_count, dtype=jnp.int32)[None, None, :]
    ).reshape(-1)
    return fold_parts(
        running,
        peak_score.reshape(-1, head_count),
        weight_sum.reshape(-1, head_count),
        weighted.reshape(-1, head_count, HD),
        row_index,
        head_count,
    )


def fresh_part(query_heads, key_heads, value_heads):
    new_count = query_heads.shape[1]
    head_count = query_heads.shape[2]
    scores = jnp.einsum(
        "rthe,ruhe->rthu", query_heads, key_heads, preferred_element_type=jnp.float32
    ) * HD ** (-0.5)
    causal = (jnp.arange(new_count)[:, None] >= jnp.arange(new_count)[None, :])[None, :, None, :]
    scores = jnp.where(causal, scores, NEG_BIG)
    peak_score = jnp.max(scores, axis=-1)
    exponent = jnp.where(causal, jnp.exp(scores - peak_score[..., None]), 0.0)
    weight_sum = jnp.sum(exponent, axis=-1)
    rounded = exponent.astype(jnp.bfloat16)
    weighted = jnp.einsum(
        "rthu,ruhe->rthe", rounded, value_heads, preferred_element_type=jnp.float32
    )
    return (
        peak_score.reshape(-1, head_count),
        weight_sum.reshape(-1, head_count),
        weighted.reshape(-1, head_count * HD),
    )


def combine_parts(first_part, second_part):
    peak_one, sum_one, acc_one = first_part
    peak_two, sum_two, acc_two = second_part
    head_count = peak_one.shape[1]
    peak_score = jnp.maximum(peak_one, peak_two)
    factor_one = jnp.exp(peak_one - peak_score)
    factor_two = jnp.exp(peak_two - peak_score)
    weight_sum = sum_one * factor_one + sum_two * factor_two
    head_width = acc_one.shape[1] // head_count
    weighted = (
        acc_one.reshape(-1, head_count, head_width) * factor_one[:, :, None]
        + acc_two.reshape(-1, head_count, head_width) * factor_two[:, :, None]
    )
    return (peak_score, weight_sum, weighted.reshape(-1, head_count * head_width))


def per_device(
    hidden,
    norm_gains,
    w_qkv,
    w_self_out,
    w_cross_q,
    w_cross_out,
    w_up,
    w_down,
    kv_cache,
    encoder_kv,
    cache_lengths,
    page_table,
    group_of,
):
    own_rows = hidden.shape[0]
    own_requests = own_rows // NEW
    local_width = w_qkv.shape[2]
    head_count = local_width // HD
    residual = hidden.astype(jnp.float32)
    normed = layer_norm(residual, norm_gains[0]).astype(jnp.bfloat16)
    own_queries = jnp.dot(normed, w_qkv[0], preferred_element_type=jnp.float32).astype(jnp.bfloat16)
    own_keys = jnp.dot(normed, w_qkv[1], preferred_element_type=jnp.float32).astype(jnp.bfloat16)
    own_values = jnp.dot(normed, w_qkv[2], preferred_element_type=jnp.float32).astype(jnp.bfloat16)
    all_queries = lax.all_gather(own_queries, "seq", axis=0, tiled=True)
    request_count = all_queries.shape[0] // NEW
    total_rows = request_count * NEW
    query_heads = all_queries.reshape(request_count, NEW, head_count, HD)
    slot_count = kv_cache.shape[1]
    first_slot = lax.axis_index("seq") * slot_count
    slot_members, valid_keys, live_pages = page_meta(
        page_table, group_of, cache_lengths, first_slot, slot_count, PAGE, GSIZE
    )
    key_pages = kv_cache[0].reshape(slot_count, PAGE, head_count, HD)
    value_pages = kv_cache[1].reshape(slot_count, PAGE, head_count, HD)

    def loop_step(block_index, running):
        block_start = block_index * 4
        return page_block(
            running,
            lax.dynamic_slice_in_dim(key_pages, block_start, 4, 0),
            lax.dynamic_slice_in_dim(value_pages, block_start, 4, 0),
            query_heads,
            lax.dynamic_slice_in_dim(slot_members, block_start, 4, 0),
            lax.dynamic_slice_in_dim(valid_keys, block_start, 4, 0),
        )

    start_state = (
        jnp.full((total_rows, head_count), NEG_BIG, jnp.float32),
        jnp.zeros((total_rows, head_count), jnp.float32),
        jnp.zeros((total_rows, local_width), jnp.float32),
    )
    cached = lax.fori_loop(0, (live_pages + 3) // 4, loop_step, start_state)
    row_start = lax.axis_index("seq") * own_rows
    merged = joined((cached[0], cached[1], cached[2]), "seq", combine_parts)
    gathered = (
        lax.dynamic_slice_in_dim(merged[0], row_start, own_rows, 0),
        lax.dynamic_slice_in_dim(merged[1], row_start, own_rows, 0),
        lax.dynamic_slice_in_dim(merged[2], row_start, own_rows, 0),
    )
    fresh = fresh_part(
        own_queries.reshape(own_requests, NEW, head_count, HD),
        own_keys.reshape(own_requests, NEW, head_count, HD),
        own_values.reshape(own_requests, NEW, head_count, HD),
    )
    peak_score, weight_sum, weighted = combine_parts(gathered, fresh)
    attended = (weighted.reshape(own_rows, head_count, HD) / weight_sum[:, :, None]).reshape(
        own_rows, local_width
    )
    attended = attended.astype(jnp.bfloat16)
    self_part = jnp.dot(attended, w_self_out, preferred_element_type=jnp.float32)
    self_mixed = residual + lax.psum(self_part, "tp")
    cross_normed = layer_norm(self_mixed, norm_gains[1]).astype(jnp.bfloat16)
    cross_queries = jnp.dot(cross_normed, w_cross_q, preferred_element_type=jnp.float32).astype(
        jnp.bfloat16
    )
    cross_queries = cross_queries.reshape(own_requests, NEW, head_count, HD)
    source_len = encoder_kv.shape[2]
    enc_keys = encoder_kv[0].reshape(own_requests, source_len, head_count, HD)
    enc_values = encoder_kv[1].reshape(own_requests, source_len, head_count, HD)
    cross_scores = jnp.einsum(
        "rthe,rshe->rths", cross_queries, enc_keys, preferred_element_type=jnp.float32
    ) * HD ** (-0.5)
    cross_peak = jnp.max(cross_scores, axis=-1, keepdims=True)
    cross_exp = jnp.exp(cross_scores - cross_peak)
    cross_probs = (cross_exp / jnp.sum(cross_exp, axis=-1, keepdims=True)).astype(jnp.bfloat16)
    context = jnp.einsum(
        "rths,rshe->rthe", cross_probs, enc_values, preferred_element_type=jnp.float32
    )
    context = context.reshape(own_rows, local_width).astype(jnp.bfloat16)
    cross_part = jnp.dot(context, w_cross_out, preferred_element_type=jnp.float32)
    cross_mixed = self_mixed + lax.psum(cross_part, "tp")
    last_normed = layer_norm(cross_mixed, norm_gains[2]).astype(jnp.bfloat16)
    hidden_units = jnp.maximum(
        jnp.dot(last_normed, w_up, preferred_element_type=jnp.float32), 0.0
    ).astype(jnp.bfloat16)
    down_part = jnp.dot(hidden_units, w_down, preferred_element_type=jnp.float32)
    own_columns = lax.psum_scatter(down_part, "tp", scatter_dimension=1, tiled=True)
    column_count = own_columns.shape[1]
    resid_part = lax.dynamic_slice_in_dim(
        cross_mixed, lax.axis_index("tp") * column_count, column_count, 1
    )
    return (resid_part + own_columns).astype(jnp.bfloat16)


def solution(mesh):
    in_specs = (
        P("seq", None),
        P(),
        P(None, None, "tp"),
        P("tp", None),
        P(None, "tp"),
        P("tp", None),
        P(None, "tp"),
        P("tp", None),
        P(None, "seq", None, "tp"),
        P(None, "seq", None, "tp"),
        P(),
        P(),
        P(),
    )
    out_specs = P("seq", "tp")
    return jax.shard_map(
        per_device, mesh=mesh, in_specs=in_specs, out_specs=out_specs, check_vma=False
    )
```

profile of v0, /device:TPU:0, one launch (start us, length us, event | category | flops | bytes accessed | tf_op | source)
XLA Modules:
  0.0 2032.0 jit_solution(12865507248875809762)
XLA Ops:
  9.6 339.2 %scatter_custom_fusion.3 = s32[97]{0:T(128)S(1)} fusion(s32[49152]{0:T(1024)S(1)} %bitcast.164, s32[49152]{0:T(1024)S(1)} %broadcast.284, s32[]{:T(128)} %constant.111.clone.1), kind=kCustom, calls=%fused_computation.153 | custom fusion | flops 49152 | bytes 392 | tf_op jit(solution)/shard_map/scatter-max | solution.py:44
  350.6 290.6 %gather_fusion.2 = s32[49152]{0:T(1024)S(1)} fusion(s32[96]{0:T(128)S(1)} %copy-done.1, s32[49152]{0:T(1024)S(1)} %broadcast_clamp_fusion), kind=kCustom, calls=%fused_computation.2 | custom fusion | bytes 589824 | tf_op jit(solution)/shard_map/gather | solution.py:41
  641.2 339.2 %scatter_custom_fusion.4 = s32[97]{0:T(128)S(1)} fusion(s32[49152]{0:T(1024)S(1)} %bitcast.165, s32[49152]{0:T(1024)S(1)} %gather_fusion.2, s32[]{:T(128)} %constant.111.clone.1), kind=kCustom, calls=%fused_computation.151 | custom fusion | flops 49152 | bytes 392 | tf_op jit(solution)/shard_map/scatter-max | solution.py:41
  980.4 339.2 %scatter_custom_fusion.5 = s32[97]{0:T(128)S(1)} fusion(s32[49152]{0:T(1024)S(1)} %bitcast.166, s32[49152]{0:T(1024)S(1)} %bitcast.163, s32[]{:T(128)} %constant.111.clone.1), kind=kCustom, calls=%fused_computation.149 | custom fusion | flops 49152 | bytes 392 | tf_op jit(solution)/shard_map/scatter-max | solution.py:39
  1324.5 6.3 gather_fusion.4
  1338.6 26.2 %all-gather.3 = bf16[32,12,256]{2,1,0:T(8,128)(2,1)S(1)} all-gather(bf16[1,12,256]{2,1,0:T(8,128)(2,1)S(1)} %bitcast.167), channel_id=1, replica_groups=mesh['seq'=32,'tp'=4] {'seq'}, dimensions={0}, use_global_device_ids=true | all-gather | bytes 202752 | tf_op jit(solution)/shard_map/all_gather | solution.py:164
  1365.8 10.5 fusion.89
  1376.2 8.7 copy.93
  1384.9 8.6 copy.94
  1395.4 402.1 %while.33 = (s32[]{:T(128)}, f32[384,4]{1,0:T(8,128)S(1)}, f32[384,4]{1,0:T(8,128)S(1)}, f32[384,256]{0,1:T(8,128)}, s32[]{:T(128)}, /*index=5*/s32[96,8]{1,0:T(...) while((s32[]{:T(128)}, f32[384,4]{1,0:T(8,128)S(1)}, ...), condition=%wide.region_13.14_spmd, body=%wide.region_7.13_spmd.sunk | while | flops 17537668 | bytes 5449411 | solution.py:192
  1406.0 4.9 scatter_fusion.1
  1424.3 4.9 scatter_fusion.1
  1442.5 4.9 scatter_fusion.1
  1460.8 4.9 scatter_fusion.1
  1479.1 4.9 scatter_fusion.1
  1497.4 4.9 scatter_fusion.1
  1607.0 4.9 scatter_fusion.1
  1625.3 4.9 scatter_fusion.1
  1661.8 4.9 scatter_fusion.1
  1680.1 4.9 scatter_fusion.1
  1698.4 4.9 scatter_fusion.1
  1734.9 4.9 scatter_fusion.1
  1771.4 4.9 scatter_fusion.1
  1789.7 4.9 scatter_fusion.1
  1799.8 55.9 %all-gather = f32[12288,4]{0,1:T(4,128)S(1)} all-gather(f32[384,4]{0,1:T(4,128)S(1)} %copy.95), channel_id=2, replica_groups=mesh['seq'=32,'tp'=4] {'seq'}, dimensions={0}, use_global_device_ids=true | all-gather | bytes 202752 | tf_op jit(solution)/shard_map/all_gather | solution.py:16
  1855.8 25.5 %all-gather.1 = f32[12288,4]{0,1:T(4,128)S(1)} all-gather(f32[384,4]{0,1:T(4,128)S(1)} %copy.96), channel_id=3, replica_groups=mesh['seq'=32,'tp'=4] {'seq'}, dimensions={0}, use_global_device_ids=true | all-gather | bytes 202752 | tf_op jit(solution)/shard_map/all_gather | solution.py:16
  1886.0 10.9 all-gather.6.cloned.1.call-done
  1898.1 65.0 %while.34 = (s32[]{:T(128)}, f32[384,4]{0,1:T(4,128)S(1)}, f32[384,4]{0,1:T(4,128)S(1)}, f32[384,256]{0,1:T(8,128)S(1)}, f32[32,384,4]{1,2,0:T(4,128)S(1)}, /*in...) while((s32[]{:T(128)}, f32[384,4]{0,1:T(4,128)S(1)}, ...), condition=%wide.region_15.16_spmd, body=%wide.region_14.15_spmd.sunk | while | flops 304133 | bytes 2814103 | solution.py:22
  1964.3 17.5 psum.14
  1984.5 14.8 psum.15
  1999.6 5.3 fusion.25
  2005.0 18.8 reduce-scatter.2.cloned.1.call-done
  (876 shorter events, 427.0 us)
Async XLA Ops:
  6.5 1957.6 %copy-start = (bf16[256,1024]{1,0:T(8,128)(2,1)S(1)}, bf16[256,1024]{1,0:T(8,128)(2,1)}, u32[]{:S(2)}) copy-start(bf16[256,1024]{1,0:T(8,128)(2,1)} %param.20) | copy-start | bytes 1572868
  6.5 344.0 %copy-start.1 = (s32[96]{0:T(128)S(1)}, s32[96]{0:T(128)}, u32[]{:S(2)}) copy-start(s32[96]{0:T(128)} %param.29) | copy-start | bytes 1156
  6.5 1890.3 %all-gather.6.cloned.1.call-start = ((), (), s32[]{:S(2)}) async-start(), calls=%async_computation.2 | async-start | bytes 12976128 | tf_op jit(solution)/shard_map/all_gather | solution.py:16
  641.2 683.3 %copy-start.3 = (s32[96,512]{1,0:T(8,128)S(1)}, s32[96,512]{1,0:T(8,128)}, u32[]{:S(2)}) copy-start(s32[96,512]{1,0:T(8,128)} %param.28) | copy-start | bytes 589828
  1330.8 0.7 copy-start.2
  1331.4 5.0 copy-start.4
  1331.4 5.3 copy-start.11
  1336.5 39.7 %copy-start.13 = (f32[12]{0:T(128)}, f32[12]{0:T(128)S(1)}, u32[]{:S(2)}) copy-start(f32[12]{0:T(128)S(1)} %broadcast_multiply_fusion.4) | copy-start | bytes 148
  1336.7 1.9 copy-start.14
  1337.3 38.9 %copy-start.12 = (f32[1,1024]{1,0:T(1,128)}, f32[1,1024]{1,0:T(1,128)S(1)}, u32[]{:S(2)}) copy-start(f32[1,1024]{1,0:T(1,128)S(1)} %get-tuple-element.316) | copy-start | bytes 12292
  1797.5 87.3 %copy-start.5 = (bf16[2,3,256,256]{3,2,1,0:T(8,128)(2,1)S(1)}, bf16[2,3,256,256]{3,2,1,0:T(8,128)(2,1)}, u32[]{:S(2)}) copy-start(bf16[2,3,256,256]{3,2,1,0:T(8,128)(2,1)} %param.26) | copy-start | bytes 2359300
  1799.6 224.3 %reduce-scatter.2.cloned.1.call-start = ((), (), s32[]{:S(2)}) async-start(), calls=%async_computation.1 | async-start | bytes 81920 | tf_op jit(solution)/shard_map/reduce_scatter | solution.py:237
  1881.2 16.9 copy-start.8
  1898.1 84.1 %copy-start.6 = (bf16[1024,256]{1,0:T(8,128)(2,1)S(1)}, bf16[1024,256]{1,0:T(8,128)(2,1)}, u32[]{:S(2)}) copy-start(bf16[1024,256]{1,0:T(8,128)(2,1)} %param.21) | copy-start | bytes 1572868
  1898.1 84.1 %copy-start.10 = (f32[1,1024]{1,0:T(1,128)S(1)}, f32[1,1024]{1,0:T(1,128)}, u32[]{:S(2)}) copy-start(f32[1,1024]{1,0:T(1,128)} %get-tuple-element.317) | copy-start | bytes 12292
  1898.1 86.2 %copy-start.7 = (bf16[256,1024]{1,0:T(8,128)(2,1)S(1)}, bf16[256,1024]{1,0:T(8,128)(2,1)}, u32[]{:S(2)}) copy-start(bf16[256,1024]{1,0:T(8,128)(2,1)} %param.22) | copy-start | bytes 1572868
  1963.1 36.5 %copy-start.9 = (f32[1,1024]{1,0:T(1,128)S(1)}, f32[1,1024]{1,0:T(1,128)}, u32[]{:S(2)}) copy-start(f32[1,1024]{1,0:T(1,128)} %get-tuple-element.315) | copy-start | bytes 12292
Sparse Core Ops, SparseCore 0:
  1799.7 97.1 all-gather.5
  2005.1 18.6 reduce-scatter.1
where the time goes:
time: 2040 us; the launch traced here: 2030 us
  other arithmetic  1260 us (62%)
  local copies, waits for them, and re-layouts  515 us (25%)
  blocking collectives  140 us (7%)
  matrix products  66.6 us (3%)
  waiting for transfers between devices  29.8 us (1%)
    another operation x1, other arithmetic, page_meta(): jnp.zeros((slot_count + 1,), jnp.int32).at[target].max(group_of[owner_ids])  339 us
    another operation x1, other arithmetic, page_meta(): jnp.zeros((slot_count + 1,), jnp.int32).at[target]  339 us
    another operation x1, other arithmetic, page_meta(): jnp.zeros((slot_count + 1,), jnp.int32).at[target].max(logical)[:slot_count]  339 us
    gather x1, local copies, waits for them, and re-layouts, page_meta(): group_of[owner_ids]  291 us
    scatter-add x22, other arithmetic, fold_parts(): new_acc = scaled_acc.at[row_index].add(weighted * factor[:, :, None]).res...  108 us
    all_gather x2, blocking collectives, joined(): everything = jax.tree.map(lambda part: lax.all_gather(part, axis), shard)  81.3 us
  transfers between devices with their start and end apart: 2, of which 2 were waited for; matrix products, arithmetic and copies ran while one was open for 0% of the time, Pallas kernels for 0%

commit v1 on v0

v1 whole, which is shorter than its diff:
```python
import functools

import jax
import jax.numpy as jnp
from jax import lax
from jax.experimental import pallas as pl
from jax.experimental.pallas import tpu as pltpu
from jax.sharding import PartitionSpec as P

HD = 64
PAGE = 128
NEW = 4
GSIZE = 8
BLOCK = 16
NEG_BIG = -1e30
FLOOR = -1e29
MESH = pl.DeviceIdType.MESH
F32 = jnp.float32
BF16 = jnp.bfloat16
NT = (((1,), (1,)), ((), ()))
TN = (((0,), (0,)), ((), ()))


def iota(shape, dim):
    return lax.broadcasted_iota(jnp.int32, shape, dim)


def dot(a, b, dims=None):
    if dims is None:
        return jnp.dot(a, b, preferred_element_type=F32)
    return lax.dot_general(a, b, dims, preferred_element_type=F32)


def layer_norm(values, gain):
    centre = values - jnp.mean(values, axis=-1, keepdims=True)
    spread = jnp.mean(centre * centre, axis=-1, keepdims=True)
    return (centre * lax.rsqrt(spread + 1e-05) * gain).astype(BF16)


def one_hot(condition):
    return jnp.where(condition, 1.0, 0.0).astype(BF16)


def kernel(
    n_seq,
    n_tp,
    hidden_h,
    gains_h,
    wqkv_h,
    wso_h,
    wcq_h,
    wco_h,
    wup_h,
    wdn_h,
    kv_h,
    enc_h,
    len_h,
    table_h,
    group_h,
    out_ref,
    hidden,
    gains,
    wqkv,
    wso,
    wcq,
    wco,
    wup,
    wdn,
    kbuf,
    vbuf,
    enc,
    lens,
    table,
    groups,
    resid,
    own,
    qall,
    table_t,
    nvalid_t,
    owners,
    nrh,
    gmat,
    scal_v,
    scal_s,
    to_dest,
    to_group,
    qbd,
    sbuf,
    mbuf,
    lbuf,
    mg,
    mparts,
    acc,
    mlsrc,
    paysrc,
    pay,
    got,
    tsend,
    trecv,
    dsend,
    drecv,
    load_sem,
    cache_sem,
    scal_sem,
    qsend_sem,
    qrecv_sem,
    psend_sem,
    precv_sem,
    tsend_sem,
    trecv_sem,
):
    own_rows, width = hidden.shape
    local = wso.shape[0]
    heads = local // HD
    slots = kbuf.shape[0]
    requests = groups.shape[1]
    group_count = requests // GSIZE
    own_requests = own_rows // NEW
    most_pages = table.shape[1]
    grows = GSIZE * NEW
    rh = heads * grows
    all_rows = n_seq * BLOCK
    sorted_rows = group_count * grows
    me = lax.axis_index("seq")
    my_tp = lax.axis_index("tp")

    loads = [
        (hidden_h, hidden),
        (gains_h, gains),
        (wqkv_h, wqkv),
        (table_h, table),
        (len_h, lens),
        (group_h, groups),
        (wso_h, wso),
        (wcq_h, wcq),
        (enc_h, enc),
        (wco_h, wco),
        (wup_h, wup),
        (wdn_h, wdn),
    ]
    copies = [
        pltpu.make_async_copy(src, dst, load_sem.at[i]) for i, (src, dst) in enumerate(loads)
    ]
    parts = 4
    span = slots // parts
    cache_copies = [
        pltpu.make_async_copy(
            kv_h.at[which, pl.ds(p * span, span)],
            buf.at[pl.ds(p * span, span)],
            cache_sem.at[which, p],
        )
        for which, buf in ((0, kbuf), (1, vbuf))
        for p in range(parts)
    ]
    for copy in copies[:6]:
        copy.start()

    barrier = pltpu.get_barrier_semaphore()

    def greet(k, carry):
        pl.semaphore_signal(
            barrier, inc=1, device_id={"seq": lax.rem(me + k, n_seq)}, device_id_type=MESH
        )
        return carry

    lax.fori_loop(1, n_seq, greet, 0)
    for k in range(1, n_tp):
        pl.semaphore_signal(
            barrier, inc=1, device_id={"tp": lax.rem(my_tp + k, n_tp)}, device_id_type=MESH
        )

    for copy in cache_copies[:parts]:
        copy.start()
    for copy in cache_copies[parts:]:
        copy.start()
    for copy in copies[6:]:
        copy.start()

    copies[0].wait()
    copies[1].wait()
    resid[...] = jnp.zeros_like(resid)
    resid[0:own_rows, :] = hidden[...].astype(F32)
    normed = layer_norm(resid[...], gains[0:1, :])
    copies[2].wait()
    queries = dot(normed, wqkv[0]).astype(BF16)
    qall[pl.ds(me * BLOCK, BLOCK), :] = queries
    own[0] = queries
    pl.semaphore_wait(barrier, n_seq + n_tp - 2)

    def query_copy(k, source):
        return pltpu.make_async_remote_copy(
            src_ref=own.at[0],
            dst_ref=qall.at[pl.ds(source * BLOCK, BLOCK), :],
            send_sem=qsend_sem.at[k],
            recv_sem=qrecv_sem.at[k],
            device_id={"seq": lax.rem(me + k, n_seq)},
            device_id_type=MESH,
        )

    def send_query(k, carry):
        query_copy(k, me).start()
        return carry

    lax.fori_loop(1, n_seq, send_query, 0)
    own[1] = dot(normed, wqkv[1]).astype(BF16)
    own[2] = dot(normed, wqkv[2]).astype(BF16)

    copies[3].wait()
    copies[4].wait()
    copies[5].wait()
    first_slot = me * slots
    eye = iota((requests, requests), 0) == iota((requests, requests), 1)
    group_row = groups[...]
    group_sq = jnp.broadcast_to(group_row, (requests, requests))
    group_col = jnp.sum(jnp.where(eye, group_sq, 0), axis=1, keepdims=True)
    earlier = iota((requests, requests), 0) < iota((requests, requests), 1)
    same = group_col == group_sq
    member_row = jnp.sum(jnp.where(same & earlier, 1, 0), axis=0, keepdims=True)
    member_sq = jnp.broadcast_to(member_row, (requests, requests))
    member_col = jnp.sum(jnp.where(eye, member_sq, 0), axis=1, keepdims=True)
    place_row = group_row * GSIZE + member_row
    place_col = group_col * GSIZE + member_col
    dest = iota((all_rows, requests), 0)
    inner = dest % BLOCK
    request_of = (dest // BLOCK) * own_requests + inner // NEW
    hit = (request_of == iota((all_rows, requests), 1)) & (inner < own_rows)
    at_col = jnp.sum(jnp.where(hit, place_row + 1, 0), axis=1, keepdims=True)
    token = iota((all_rows, 1), 0) % NEW
    at_col = jnp.where(at_col > 0, (at_col - 1) * NEW + token, -1)
    dest_t = iota((requests, all_rows), 1)
    inner_t = dest_t % BLOCK
    request_t = (dest_t // BLOCK) * own_requests + inner_t // NEW
    hit_t = (request_t == iota((requests, all_rows), 0)) & (inner_t < own_rows)
    at_row = jnp.sum(jnp.where(hit_t, place_col + 1, 0), axis=0, keepdims=True)
    token_t = iota((1, all_rows), 1) % NEW
    at_row = jnp.where(at_row > 0, (at_row - 1) * NEW + token_t, -1)
    to_dest[...] = one_hot(at_col == iota((all_rows, sorted_rows), 1))
    to_group[...] = one_hot(at_row == iota((sorted_rows, all_rows), 0))

    table_t[...] = jnp.transpose(table[...] - first_slot)
    page_at = iota((most_pages, requests), 0)
    nvalid_t[...] = jnp.clip(lens[...] - page_at * PAGE, 0, PAGE)
    unroll = 8

    def match(i, carry):
        slot0 = i * unroll

        def over_pages(j, sums):
            rows = pl.ds(pl.multiple_of(j * 8, 8), 8)
            at = table_t[rows, :]
            count = nvalid_t[rows, :]
            return tuple(jnp.where(at == slot0 + u, count, sums[u]) for u in range(unroll))

        sums = lax.fori_loop(
            0,
            most_pages // 8,
            over_pages,
            tuple(jnp.zeros((8, requests), jnp.int32) for _ in range(unroll)),
            unroll=4,
        )
        for u in range(unroll):
            owners[pl.ds(slot0 + u, 1), :] = jnp.max(sums[u], axis=0, keepdims=True)
        return carry

    lax.fori_loop(0, slots // unroll, match, 0)
    owner = owners[...]
    lane_member = (iota((requests, rh), 1) % grows) // NEW
    nrh[...] = dot(owner.astype(F32).astype(BF16), one_hot(member_col == lane_member))
    slot_group = jnp.max(jnp.where(owner > 0, group_row, -1), axis=1, keepdims=True)
    gmat[...] = jnp.broadcast_to(slot_group, (slots, rh))
    eye_s = iota((slots, slots), 0) == iota((slots, slots), 1)
    group_at = jnp.sum(
        jnp.where(eye_s, jnp.broadcast_to(slot_group, (slots, slots)), 0), axis=0, keepdims=True
    )
    before = (iota((slots, slots), 0) < iota((slots, slots), 1)) & (slot_group == group_at)
    before = before & (slot_group >= 0)
    previous = jnp.max(jnp.where(before, iota((slots, slots), 0), -1), axis=0, keepdims=True)
    mine = slot_group == iota((slots, 128), 1)
    last = jnp.max(jnp.where(mine, iota((slots, 128), 0), -1), axis=0, keepdims=True)
    scal_v[...] = jnp.zeros_like(scal_v)
    scal_v[0:1, 0:slots] = jnp.clip(group_at, 0, group_count - 1)
    scal_v[1:2, 0:slots] = jnp.where(previous < 0, slots, previous)
    scal_v[2:3, :] = jnp.where(last < 0, slots, last)
    scalars = pltpu.make_async_copy(scal_v, scal_s, scal_sem)
    scalars.start()

    def wait_query(k, carry):
        query_copy(k, lax.rem(me + n_seq - k, n_seq)).wait_recv()
        return carry

    lax.fori_loop(1, n_seq, wait_query, 0)
    sorted_queries = dot(to_group[...], qall[...]) * HD ** (-0.5)
    row_head = iota((grows, local), 1) // HD
    for g in range(group_count):
        block = sorted_queries[g * grows : (g + 1) * grows, :]
        for h in range(heads):
            qbd[g, h * grows : (h + 1) * grows, :] = jnp.where(row_head == h, block, 0.0).astype(
                BF16
            )
    scalars.wait()

    for copy in cache_copies[:parts]:
        copy.wait()
    key_at = iota((PAGE, rh), 0).astype(F32)
    step = 4

    def group_of_slot(s):
        return jnp.clip(scal_s[0, s], 0, group_count - 1)

    def acc_slot(row, at):
        return jnp.clip(scal_s[row, at], 0, slots)

    def score(i, carry):
        for u in range(step):
            s = i * step + u
            scores = dot(kbuf[s], qbd[group_of_slot(s)], NT)
            scores = jnp.where(key_at < nrh[pl.ds(s, 1), :], scores, NEG_BIG)
            sbuf[s] = scores
            mbuf[pl.ds(s, 1), :] = jnp.max(scores, axis=0, keepdims=True)
        return carry

    lax.fori_loop(0, slots // step, score, 0)
    for g in range(group_count):
        peak = jnp.max(jnp.where(gmat[...] == g, mbuf[...], NEG_BIG), axis=0, keepdims=True)
        peak = jnp.maximum(peak, FLOOR)
        high = peak.astype(BF16)
        low = (peak - high.astype(F32)).astype(BF16)
        mparts[0, g : g + 1, :] = high.astype(F32)
        mparts[1, g : g + 1, :] = low.astype(F32)
        mg[g] = jnp.broadcast_to(high.astype(F32) + low.astype(F32), (8, rh))

    for copy in cache_copies[parts:]:
        copy.wait()
    acc[slots] = jnp.zeros((grows, local), F32)

    def weigh(i, carry):
        for u in range(step):
            s = i * step + u
            peak = mg[group_of_slot(s)][0:1, :]
            weights = jnp.exp(sbuf[s] - peak)
            lbuf[pl.ds(s, 1), :] = jnp.sum(weights, axis=0, keepdims=True)
            product = dot(weights.astype(BF16), vbuf[s], TN)
            picked = product[0:grows, :]
            for h in range(1, heads):
                picked = jnp.where(row_head == h, product[h * grows : (h + 1) * grows, :], picked)
            acc[s] = picked + acc[acc_slot(1, s)]
        return carry

    lax.fori_loop(0, slots // step, weigh, 0)

    diagonal = (iota((grows, rh), 1) % grows) == iota((grows, rh), 0)
    for g in range(group_count):
        rows = slice(g * grows, (g + 1) * grows)
        total = jnp.sum(jnp.where(gmat[...] == g, lbuf[...], 0.0), axis=0, keepdims=True)
        high = total.astype(BF16).astype(F32)
        pieces = (mparts[0, g : g + 1, :], mparts[1, g : g + 1, :], high, total - high)
        for p, piece in enumerate(pieces):
            mlsrc[rows, p * rh : (p + 1) * rh] = jnp.where(diagonal, piece, 0.0).astype(BF16)
        paysrc[rows, 0:local] = acc[acc_slot(2, g)].astype(BF16)
    source = iota((4 * rh, 128), 0)
    spread = one_hot(
        iota((4 * rh, 128), 1) == (source // rh) * heads + (source % rh) // grows
    )
    paysrc[:, local:] = dot(mlsrc[...], spread).astype(BF16)
    pay[...] = dot(to_dest[...], paysrc[...]).astype(BF16)
    got[pl.ds(me * BLOCK, BLOCK), :] = pay[pl.ds(me * BLOCK, BLOCK), :]

    def part_copy(k, target, source):
        return pltpu.make_async_remote_copy(
            src_ref=pay.at[pl.ds(target * BLOCK, BLOCK), :],
            dst_ref=got.at[pl.ds(source * BLOCK, BLOCK), :],
            send_sem=psend_sem.at[k],
            recv_sem=precv_sem.at[k],
            device_id={"seq": target},
            device_id_type=MESH,
        )

    def send_part(k, carry):
        part_copy(k, lax.rem(me + k, n_seq), me).start()
        return carry

    lax.fori_loop(1, n_seq, send_part, 0)

    q_new = own[0].astype(F32) * HD ** (-0.5)
    k_new = own[1].astype(F32)
    v_new = own[2].astype(F32)
    same_head = one_hot(iota((local, local), 0) // HD == iota((local, local), 1) // HD)
    product = jnp.concatenate(
        [q_new * (pltpu.roll(k_new, d, 0) if d else k_new) for d in range(NEW)], axis=0
    )
    high = product.astype(BF16)
    low = (product - high.astype(F32)).astype(BF16)
    new_scores = dot(high, same_head) + dot(low, same_head)
    token_at = iota((BLOCK, local), 0) % NEW
    new_scores = [
        jnp.where(token_at >= d, new_scores[d * BLOCK : (d + 1) * BLOCK, :], NEG_BIG)
        for d in range(NEW)
    ]
    new_peak = functools.reduce(jnp.maximum, new_scores)
    new_weights = [jnp.exp(scores - new_peak) for scores in new_scores]
    new_total = functools.reduce(jnp.add, new_weights)
    new_sum = functools.reduce(
        jnp.add,
        [
            new_weights[d].astype(BF16).astype(F32) * (pltpu.roll(v_new, d, 0) if d else v_new)
            for d in range(NEW)
        ],
    )

    def wait_part(k, carry):
        part_copy(k, lax.rem(me + k, n_seq), lax.rem(me + n_seq - k, n_seq)).wait_recv()
        return carry

    lax.fori_loop(1, n_seq, wait_part, 0)
    lane = iota((128, local), 0)
    column_head = iota((128, local), 1) // HD
    pick_peak = one_hot((lane < 2 * heads) & (lane % heads == column_head))
    pick_total = one_hot(
        (lane >= 2 * heads) & (lane < 4 * heads) & (lane % heads == column_head)
    )
    peaks = dot(got[:, local:], pick_peak).reshape(n_seq, BLOCK, local)
    totals = dot(got[:, local:], pick_total).reshape(n_seq, BLOCK, local)
    sums = got[:, 0:local].astype(F32).reshape(n_seq, BLOCK, local)
    peak = jnp.maximum(jnp.max(peaks, axis=0), new_peak)
    factor = jnp.exp(peaks - peak[None])
    new_factor = jnp.exp(new_peak - peak)
    total = jnp.sum(totals * factor, axis=0) + new_total * new_factor
    weighted = jnp.sum(sums * factor, axis=0) + new_sum * new_factor
    attended = (weighted / total).astype(BF16)

    def tp_copies(stage):
        return [
            pltpu.make_async_remote_copy(
                src_ref=tsend.at[stage],
                dst_ref=trecv.at[stage, k - 1],
                send_sem=tsend_sem.at[stage, k - 1],
                recv_sem=trecv_sem.at[stage, k - 1],
                device_id={"tp": lax.rem(my_tp + k, n_tp)},
                device_id_type=MESH,
            )
            for k in range(1, n_tp)
        ]

    def tp_sum(part, stage):
        tsend[stage] = part.astype(BF16)
        sent = tp_copies(stage)
        for copy in sent:
            copy.start()
        for copy in sent:
            copy.wait()
        for k in range(n_tp - 1):
            part = part + trecv[stage, k].astype(F32)
        return part

    copies[6].wait()
    self_mixed = resid[...] + tp_sum(dot(attended, wso[...]), 0)

    copies[7].wait()
    copies[8].wait()
    cross_normed = layer_norm(self_mixed, gains[1:2, :])
    cross_queries = dot(cross_normed, wcq[...]).astype(BF16).astype(F32) * HD ** (-0.5)
    head_of = iota((BLOCK, local), 1) // HD
    stacked = jnp.concatenate(
        [jnp.where(head_of == h, cross_queries, 0.0) for h in range(heads)], axis=0
    ).astype(BF16)
    sources = enc.shape[2]
    enc_keys = enc[0].reshape(own_requests * sources, local)
    enc_values = enc[1].reshape(own_requests * sources, local)
    cross_scores = dot(stacked, enc_keys, NT)
    shape = cross_scores.shape
    ours = iota(shape, 1) // sources == (iota(shape, 0) % BLOCK) // NEW
    cross_scores = jnp.where(ours, cross_scores, NEG_BIG)
    cross_exp = jnp.exp(cross_scores - jnp.max(cross_scores, axis=-1, keepdims=True))
    cross_probs = (cross_exp / jnp.sum(cross_exp, axis=-1, keepdims=True)).astype(BF16)
    mixed = dot(cross_probs, enc_values)
    context = mixed[0:BLOCK, :]
    for h in range(1, heads):
        context = jnp.where(head_of == h, mixed[h * BLOCK : (h + 1) * BLOCK, :], context)
    copies[9].wait()
    cross_mixed = self_mixed + tp_sum(dot(context.astype(BF16), wco[...]), 1)

    resid[...] = cross_mixed
    last_normed = layer_norm(cross_mixed, gains[2:3, :])
    copies[10].wait()
    units = jnp.maximum(dot(last_normed, wup[...]), 0.0).astype(BF16)
    copies[11].wait()
    down = dot(units, wdn[...])
    for t in range(n_tp):
        dsend[t] = down[:, t * local : (t + 1) * local]
    sent = []
    for k in range(1, n_tp):
        target = lax.rem(my_tp + k, n_tp)
        sent.append(
            pltpu.make_async_remote_copy(
                src_ref=dsend.at[target],
                dst_ref=drecv.at[k - 1],
                send_sem=tsend_sem.at[2, k - 1],
                recv_sem=trecv_sem.at[2, k - 1],
                device_id={"tp": target},
                device_id_type=MESH,
            )
        )
    for copy in sent:
        copy.start()
    total = resid[:, pl.ds(pl.multiple_of(my_tp * local, 128), local)] + dsend[my_tp]
    for k, copy in enumerate(sent):
        copy.wait()
        total = total + drecv[k]
    out_ref[...] = total[0:own_rows, :].astype(BF16)

    def wait_sends(k, carry):
        query_copy(k, me).wait_send()
        part_copy(k, lax.rem(me + k, n_seq), me).wait_send()
        return carry

    lax.fori_loop(1, n_seq, wait_sends, 0)


def solution(mesh):
    n_seq = mesh.shape["seq"]
    n_tp = mesh.shape["tp"]

    def per_device(
        hidden,
        norm_gains,
        w_qkv,
        w_self_out,
        w_cross_q,
        w_cross_out,
        w_up,
        w_down,
        kv_cache,
        encoder_kv,
        cache_lengths,
        page_table,
        group_of,
    ):
        own_rows, width = hidden.shape
        local = w_self_out.shape[0]
        heads = local // HD
        slots = kv_cache.shape[1]
        requests, most_pages = page_table.shape
        group_count = requests // GSIZE
        grows = GSIZE * NEW
        rh = heads * grows
        all_rows = n_seq * BLOCK
        sorted_rows = group_count * grows
        lens = cache_lengths.reshape(1, requests)
        groups = group_of.reshape(1, requests)

        def vmem(shape, dtype):
            return pltpu.VMEM(shape, dtype)

        def like(x, shape=None):
            return pltpu.VMEM(shape or x.shape, x.dtype)

        dma = pltpu.SemaphoreType.DMA
        scratch = [
            like(hidden),
            like(norm_gains),
            like(w_qkv),
            like(w_self_out),
            like(w_cross_q),
            like(w_cross_out),
            like(w_up),
            like(w_down),
            like(kv_cache, kv_cache.shape[1:]),
            like(kv_cache, kv_cache.shape[1:]),
            like(encoder_kv),
            like(lens),
            like(page_table),
            like(groups),
            vmem((BLOCK, width), F32),
            vmem((3, BLOCK, local), BF16),
            vmem((all_rows, local), BF16),
            vmem((most_pages, requests), jnp.int32),
            vmem((most_pages, requests), jnp.int32),
            vmem((slots, requests), jnp.int32),
            vmem((slots, rh), F32),
            vmem((slots, rh), jnp.int32),
            vmem((8, 128), jnp.int32),
            pltpu.SMEM((8, 128), jnp.int32),
            vmem((all_rows, sorted_rows), BF16),
            vmem((sorted_rows, all_rows), BF16),
            vmem((group_count, rh, local), BF16),
            vmem((slots, PAGE, rh), F32),
            vmem((slots, rh), F32),
            vmem((slots, rh), F32),
            vmem((group_count, 8, rh), F32),
            vmem((2, group_count, rh), F32),
            vmem((slots + 1, grows, local), F32),
            vmem((sorted_rows, 4 * rh), BF16),
            vmem((sorted_rows, local + 128), BF16),
            vmem((all_rows, local + 128), BF16),
            vmem((all_rows, local + 128), BF16),
            vmem((2, BLOCK, width), BF16),
            vmem((2, n_tp - 1, BLOCK, width), BF16),
            vmem((n_tp, BLOCK, local), F32),
            vmem((n_tp - 1, BLOCK, local), F32),
            dma((12,)),
            dma((2, 4)),
            dma,
            dma((n_seq,)),
            dma((n_seq,)),
            dma((n_seq,)),
            dma((n_seq,)),
            dma((3, n_tp - 1)),
            dma((3, n_tp - 1)),
        ]
        return pl.pallas_call(
            functools.partial(kernel, n_seq, n_tp),
            out_shape=jax.ShapeDtypeStruct((own_rows, local), BF16),
            in_specs=[pl.BlockSpec(memory_space=pl.ANY)] * 13,
            out_specs=pl.BlockSpec(memory_space=pltpu.VMEM),
            scratch_shapes=scratch,
            compiler_params=pltpu.CompilerParams(
                collective_id=0, has_side_effects=True, vmem_limit_bytes=60 << 20
            ),
        )(
            hidden,
            norm_gains,
            w_qkv,
            w_self_out,
            w_cross_q,
            w_cross_out,
            w_up,
            w_down,
            kv_cache,
            encoder_kv,
            lens,
            page_table,
            groups,
        )

    in_specs = (
        P("seq", None),
        P(),
        P(None, None, "tp"),
        P("tp", None),
        P(None, "tp"),
        P("tp", None),
        P(None, "tp"),
        P("tp", None),
        P(None, "seq", None, "tp"),
        P(None, "seq", None, "tp"),
        P(),
        P(),
        P(),
    )
    return jax.shard_map(
        per_device, mesh=mesh, in_specs=in_specs, out_specs=P("seq", "tp"), check_vma=False
    )
```

time: 2040 us -> 54.4 us (0.03)
  other arithmetic: 1260 us -> 0 us
  local copies, waits for them, and re-layouts: 515 us -> 1.3 us
  blocking collectives: 140 us -> 0 us
  matrix products: 66.6 us -> 0 us
  Pallas kernels: 0 us -> 52.9 us
  waiting for transfers between devices: 29.8 us -> 0 us
    another operation x25 -> x0, other arithmetic: 1050 us -> none  [the longest x1 339 us: page_meta(): jnp.zeros((slot_count + 1,), jnp.int32).at[target].max(group_of[owner_ids])]
    gather x50 -> x0, local copies, waits for them, and re-layouts: 354 us -> none  [the longest x1 291 us: page_meta(): group_of[owner_ids]]
    scatter-add x44 -> x0, other arithmetic: 138 us -> none  [the longest x22 108 us: fold_parts(): new_acc = scaled_acc.at[row_index].add(weighted * factor[:, :, None]).res...]
    all_gather x3 -> x0, blocking collectives: 108 us -> none  [the longest x2 81.3 us: joined(): everything = jax.tree.map(lambda part: lax.all_gather(part, axis), shard)]
    dot_general x55 -> x0, matrix products: 66.6 us -> none  [the longest x22 28 us: page_block(): jnp.einsum('sgthk,skhe->sgthe', rounded, page_values, preferred_element_t...]
    pallas_call x0 -> x1, Pallas kernels: none -> 52.9 us  [per_device(): pl.pallas_call(functools.partial(kernel, n_seq, n_tp), out_shape=jax.Shap...]
    dynamic_slice x84 -> x0, local copies, waits for them, and re-layouts: 51.9 us -> none  [the longest x62 36.8 us: step(): return combine(so_far, jax.tree.map(lambda part: part[k], everything))]
    psum x2 -> x0, blocking collectives: 32.3 us -> none  [the longest x1 17.5 us: per_device(): self_mixed = residual + lax.psum(self_part, 'tp')]
  transfers between devices with their start and end apart: 2 -> 0, of which waited for: 2 -> 0; matrix products, arithmetic and copies ran while one was open for 0% -> 0% of each run, Pallas kernels for 0% -> 0%
where the time goes in v1:
time: 54.4 us; the launch traced here: 54.2 us
  Pallas kernels  52.9 us (97%)
  local copies, waits for them, and re-layouts  1.3 us (2%)
    pallas_call x1, Pallas kernels, per_device(): pl.pallas_call(functools.partial(kernel, n_seq, n_tp), out_shape=jax.Shap...  52.9 us
    unnamed x1, local copies, waits for them, and re-layouts  1.3 us

profile of v1, /device:TPU:0, one launch (start us, length us, event | category | flops | bytes accessed | tf_op | source)
XLA Modules:
  0.0 54.2 jit_solution(9363959398272795444)
XLA Ops:
  0.0 52.9 %shard_map.127 = bf16[12,256]{1,0:T(8,128)(2,1)} custom-call(bf16[12,1024]{1,0:T(8,128)(2,1)} %hidden_h.1, f32[3,1024]{1,0:T(4,128)} %gains_h.1, bf16[3,1024,256]{2,1,0:T(8,128)(2,1)} %wqkv_h.1, bf16[256,1024]{1,0:T(8,128)(2,1)} %wso_h.1, bf16[1024,256]{1,0:T(8,128)(2,1)} %wcq_h.1, bf16[256,1024]{1,0:T(8,128)(2,1)} %wco_h.1, bf16[1024,2048]{1,0:T(8,128)(2,1)} %wup_h.1, ...), custom_call_target="tpu_custom_call" | custom-call | tf_op jit(solution)/shard_map/pallas_call | solution.py:610
  52.9 1.3 %copy.15 = bf16[12,256]{1,0:T(8,128)(2,1)} copy(bf16[12,256]{1,0:T(8,128)(2,1)} %shard_map.127) | data formatting | bytes 12288

commit v2 on v1

--- a/solution.py
+++ b/solution.py
@@ -35,6 +35,28 @@
     centre = values - jnp.mean(values, axis=-1, keepdims=True)
     spread = jnp.mean(centre * centre, axis=-1, keepdims=True)
     return (centre * lax.rsqrt(spread + 1e-05) * gain).astype(BF16)
+
+
+def partners(me, n_seq):
+    side = 4 if n_seq % 32 == 0 else 1
+    depth = n_seq // (2 * side)
+    x, z, core = me // (2 * depth), (me // 2) % depth, me % 2
+
+    def turn(at, by, size):
+        return jnp.where(at + by >= size, at + by - size, at + by)
+
+    def hops(offset):
+        dx, dz, _ = offset
+        return min(dx, side - dx) + min(dz, depth - dz)
+
+    offsets = [(dx, dz, dc) for dx in range(side) for dz in range(depth) for dc in range(2)][1:]
+    found = []
+    for dx, dz, dc in sorted(offsets, key=lambda offset: -hops(offset)):
+        c = 1 - core if dc else core
+        to = (turn(x, dx, side) * depth + turn(z, dz, depth)) * 2 + c
+        back = (turn(x, (side - dx) % side, side) * depth + turn(z, (depth - dz) % depth, depth)) * 2 + c
+        found.append((to, back))
+    return found
 
 
 def one_hot(condition):
@@ -123,6 +145,8 @@
     sorted_rows = group_count * grows
     me = lax.axis_index("seq")
     my_tp = lax.axis_index("tp")
+    seq_partners = partners(me, n_seq)
+    tp_steps = sorted(range(1, n_tp), key=lambda k: -min(k, n_tp - k))
 
     loads = [
         (hidden_h, hidden),
@@ -157,14 +181,9 @@
 
     barrier = pltpu.get_barrier_semaphore()
 
-    def greet(k, carry):
-        pl.semaphore_signal(
-            barrier, inc=1, device_id={"seq": lax.rem(me + k, n_seq)}, device_id_type=MESH
-        )
-        return carry
-
-    lax.fori_loop(1, n_seq, greet, 0)
-    for k in range(1, n_tp):
+    for target, _ in seq_partners:
+        pl.semaphore_signal(barrier, inc=1, device_id={"seq": target}, device_id_type=MESH)
+    for k in tp_steps:
         pl.semaphore_signal(
             barrier, inc=1, device_id={"tp": lax.rem(my_tp + k, n_tp)}, device_id_type=MESH
         )
@@ -187,21 +206,18 @@
     own[0] = queries
     pl.semaphore_wait(barrier, n_seq + n_tp - 2)
 
-    def query_copy(k, source):
+    def query_copy(k, target, source):
         return pltpu.make_async_remote_copy(
             src_ref=own.at[0],
             dst_ref=qall.at[pl.ds(source * BLOCK, BLOCK), :],
             send_sem=qsend_sem.at[k],
             recv_sem=qrecv_sem.at[k],
-            device_id={"seq": lax.rem(me + k, n_seq)},
+            device_id={"seq": target},
             device_id_type=MESH,
         )
 
-    def send_query(k, carry):
-        query_copy(k, me).start()
-        return carry
-
-    lax.fori_loop(1, n_seq, send_query, 0)
+    for k, (target, _) in enumerate(seq_partners):
+        query_copy(k, target, me).start()
     own[1] = dot(normed, wqkv[1]).astype(BF16)
     own[2] = dot(normed, wqkv[2]).astype(BF16)
 
@@ -284,11 +300,8 @@
     scalars = pltpu.make_async_copy(scal_v, scal_s, scal_sem)
     scalars.start()
 
-    def wait_query(k, carry):
-        query_copy(k, lax.rem(me + n_seq - k, n_seq)).wait_recv()
-        return carry
-
-    lax.fori_loop(1, n_seq, wait_query, 0)
+    for k, (target, source) in enumerate(seq_partners):
+        query_copy(k, target, source).wait_recv()
     sorted_queries = dot(to_group[...], qall[...]) * HD ** (-0.5)
     row_head = iota((grows, local), 1) // HD
     for g in range(group_count):
@@ -302,7 +315,7 @@
     for copy in cache_copies[:parts]:
         copy.wait()
     key_at = iota((PAGE, rh), 0).astype(F32)
-    step = 4
+    step = 32 if slots % 32 == 0 else 16
 
     def group_of_slot(s):
         return jnp.clip(scal_s[0, s], 0, group_count - 1)
@@ -357,12 +370,21 @@
         for p, piece in enumerate(pieces):
             mlsrc[rows, p * rh : (p + 1) * rh] = jnp.where(diagonal, piece, 0.0).astype(BF16)
         paysrc[rows, 0:local] = acc[acc_slot(2, g)].astype(BF16)
-    source = iota((4 * rh, 128), 0)
+    per_part = BLOCK * heads
+    source = iota((4 * rh, local), 0)
+    lane = iota((4 * rh, local), 1)
     spread = one_hot(
-        iota((4 * rh, 128), 1) == (source // rh) * heads + (source % rh) // grows
+        (lane // per_part == source // rh) & (lane % heads == (source % rh) // grows)
     )
     paysrc[:, local:] = dot(mlsrc[...], spread).astype(BF16)
-    pay[...] = dot(to_dest[...], paysrc[...]).astype(BF16)
+    both = dot(to_dest[...], paysrc[...])
+    row_in = iota((BLOCK, local), 0)
+    own_lane = ((iota((BLOCK, local), 1) % per_part) // heads == row_in)[None]
+    small = jnp.where(own_lane, both[:, local:].reshape(n_seq, BLOCK, local), 0.0)
+    small = jnp.sum(small, axis=1, keepdims=True)
+    large = both[:, 0:local].reshape(n_seq, BLOCK, local)
+    filled = jnp.where((row_in == own_rows)[None], small, large)
+    pay[...] = filled.reshape(all_rows, local).astype(BF16)
     got[pl.ds(me * BLOCK, BLOCK), :] = pay[pl.ds(me * BLOCK, BLOCK), :]
 
     def part_copy(k, target, source):
@@ -375,11 +397,8 @@
             device_id_type=MESH,
         )
 
-    def send_part(k, carry):
-        part_copy(k, lax.rem(me + k, n_seq), me).start()
-        return carry
-
-    lax.fori_loop(1, n_seq, send_part, 0)
+    for k, (target, _) in enumerate(seq_partners):
+        part_copy(k, target, me).start()
 
     q_new = own[0].astype(F32) * HD ** (-0.5)
     k_new = own[1].astype(F32)
@@ -407,26 +426,23 @@
         ],
     )
 
-    def wait_part(k, carry):
-        part_copy(k, lax.rem(me + k, n_seq), lax.rem(me + n_seq - k, n_seq)).wait_recv()
-        return carry
-
-    lax.fori_loop(1, n_seq, wait_part, 0)
-    lane = iota((128, local), 0)
-    column_head = iota((128, local), 1) // HD
-    pick_peak = one_hot((lane < 2 * heads) & (lane % heads == column_head))
-    pick_total = one_hot(
-        (lane >= 2 * heads) & (lane < 4 * heads) & (lane % heads == column_head)
-    )
-    peaks = dot(got[:, local:], pick_peak).reshape(n_seq, BLOCK, local)
-    totals = dot(got[:, local:], pick_total).reshape(n_seq, BLOCK, local)
-    sums = got[:, 0:local].astype(F32).reshape(n_seq, BLOCK, local)
+    for k, (target, source) in enumerate(seq_partners):
+        part_copy(k, target, source).wait_recv()
+    sums = got[...].astype(F32).reshape(n_seq, BLOCK, local)
+    small = jnp.where(own_lane, sums[:, own_rows : own_rows + 1, :], 0.0)
+    small = small.reshape(all_rows, local).astype(BF16)
+    lane = iota((local, local), 0)
+    column_head = lane % heads == iota((local, local), 1) // HD
+    pick_peak = one_hot((lane < 2 * per_part) & column_head)
+    pick_total = one_hot((lane >= 2 * per_part) & column_head)
+    peaks = dot(small, pick_peak).reshape(n_seq, BLOCK, local)
+    totals = dot(small, pick_total).reshape(n_seq, BLOCK, local)
     peak = jnp.maximum(jnp.max(peaks, axis=0), new_peak)
     factor = jnp.exp(peaks - peak[None])
     new_factor = jnp.exp(new_peak - peak)
     total = jnp.sum(totals * factor, axis=0) + new_total * new_factor
     weighted = jnp.sum(sums * factor, axis=0) + new_sum * new_factor
-    attended = (weighted / total).astype(BF16)
+    attended = jnp.where(row_in < own_rows, weighted / total, 0.0).astype(BF16)
 
     def tp_copies(stage):
         return [
@@ -438,7 +454,7 @@
                 device_id={"tp": lax.rem(my_tp + k, n_tp)},
                 device_id_type=MESH,
             )
-            for k in range(1, n_tp)
+            for k in tp_steps
         ]
 
     def tp_sum(part, stage):
@@ -486,9 +502,9 @@
     copies[11].wait()
     down = dot(units, wdn[...])
     for t in range(n_tp):
-        dsend[t] = down[:, t * local : (t + 1) * local]
+        dsend[t] = down[:, t * local : (t + 1) * local].astype(BF16)
     sent = []
-    for k in range(1, n_tp):
+    for k in tp_steps:
         target = lax.rem(my_tp + k, n_tp)
         sent.append(
             pltpu.make_async_remote_copy(
@@ -502,18 +518,16 @@
         )
     for copy in sent:
         copy.start()
-    total = resid[:, pl.ds(pl.multiple_of(my_tp * local, 128), local)] + dsend[my_tp]
-    for k, copy in enumerate(sent):
+    total = resid[:, pl.ds(pl.multiple_of(my_tp * local, 128), local)] + dsend[my_tp].astype(F32)
+    for copy in sent:
         copy.wait()
-        total = total + drecv[k]
+    for k in range(n_tp - 1):
+        total = total + drecv[k].astype(F32)
     out_ref[...] = total[0:own_rows, :].astype(BF16)
 
-    def wait_sends(k, carry):
-        query_copy(k, me).wait_send()
-        part_copy(k, lax.rem(me + k, n_seq), me).wait_send()
-        return carry
-
-    lax.fori_loop(1, n_seq, wait_sends, 0)
+    for k, (target, _) in enumerate(seq_partners):
+        query_copy(k, target, me).wait_send()
+        part_copy(k, target, me).wait_send()
 
 
 def solution(mesh):
@@ -590,13 +604,13 @@
             vmem((2, group_count, rh), F32),
             vmem((slots + 1, grows, local), F32),
             vmem((sorted_rows, 4 * rh), BF16),
-            vmem((sorted_rows, local + 128), BF16),
-            vmem((all_rows, local + 128), BF16),
-            vmem((all_rows, local + 128), BF16),
+            vmem((sorted_rows, 2 * local), BF16),
+            vmem((all_rows, local), BF16),
+            vmem((all_rows, local), BF16),
             vmem((2, BLOCK, width), BF16),
             vmem((2, n_tp - 1, BLOCK, width), BF16),
-            vmem((n_tp, BLOCK, local), F32),
-            vmem((n_tp - 1, BLOCK, local), F32),
+            vmem((n_tp, BLOCK, local), BF16),
+            vmem((n_tp - 1, BLOCK, local), BF16),
             dma((12,)),
             dma((2, 4)),
             dma,

time: 54.4 us -> 43.5 us (0.80)
  Pallas kernels: 52.9 us -> 42.1 us
    pallas_call x1, Pallas kernels: 52.9 us -> 42.1 us  [per_device(): pl.pallas_call(functools.partial(kernel, n_seq, n_tp), out_shape=jax.Shap...]
where the time goes in v2:
time: 43.5 us; the launch traced here: 43.4 us
  Pallas kernels  42.1 us (97%)
  local copies, waits for them, and re-layouts  1.3 us (3%)
    pallas_call x1, Pallas kernels, per_device(): pl.pallas_call(functools.partial(kernel, n_seq, n_tp), out_shape=jax.Shap...  42.1 us
    unnamed x1, local copies, waits for them, and re-layouts  1.3 us

profile of v2, /device:TPU:0, one launch (start us, length us, event | category | flops | bytes accessed | tf_op | source)
XLA Modules:
  0.0 43.4 jit_solution(6037876374179365228)
XLA Ops:
  0.0 42.1 %shard_map.127 = bf16[12,256]{1,0:T(8,128)(2,1)} custom-call(bf16[12,1024]{1,0:T(8,128)(2,1)} %hidden_h.1, f32[3,1024]{1,0:T(4,128)} %gains_h.1, bf16[3,1024,256]{2,1,0:T(8,128)(2,1)} %wqkv_h.1, bf16[256,1024]{1,0:T(8,128)(2,1)} %wso_h.1, bf16[1024,256]{1,0:T(8,128)(2,1)} %wcq_h.1, bf16[256,1024]{1,0:T(8,128)(2,1)} %wco_h.1, bf16[1024,2048]{1,0:T(8,128)(2,1)} %wup_h.1, ...), custom_call_target="tpu_custom_call" | custom-call | tf_op jit(solution)/shard_map/pallas_call | solution.py:624
  42.1 1.3 %copy.15 = bf16[12,256]{1,0:T(8,128)(2,1)} copy(bf16[12,256]{1,0:T(8,128)(2,1)} %shard_map.127) | data formatting | bytes 12288

commit v3 on v2

--- a/solution.py
+++ b/solution.py
@@ -315,7 +315,7 @@
     for copy in cache_copies[:parts]:
         copy.wait()
     key_at = iota((PAGE, rh), 0).astype(F32)
-    step = 32 if slots % 32 == 0 else 16
+    step = 48 if slots % 48 == 0 else 16
 
     def group_of_slot(s):
         return jnp.clip(scal_s[0, s], 0, group_count - 1)
@@ -457,19 +457,26 @@
             for k in tp_steps
         ]
 
+    half = width // 2
+
     def tp_sum(part, stage):
-        tsend[stage] = part.astype(BF16)
+        tsend[stage, 0:own_rows, :] = part[0:own_rows, 0:half].astype(BF16)
+        tsend[stage, own_rows : 2 * own_rows, :] = part[0:own_rows, half:].astype(BF16)
         sent = tp_copies(stage)
         for copy in sent:
             copy.start()
         for copy in sent:
             copy.wait()
-        for k in range(n_tp - 1):
-            part = part + trecv[stage, k].astype(F32)
-        return part
+        others = functools.reduce(
+            jnp.add, [trecv[stage, k].astype(F32) for k in range(n_tp - 1)]
+        )
+        resid[...] += part
+        resid[0:own_rows, 0:half] += others[0:own_rows, :]
+        resid[0:own_rows, half:] += others[own_rows:, :]
+        return resid[...]
 
     copies[6].wait()
-    self_mixed = resid[...] + tp_sum(dot(attended, wso[...]), 0)
+    self_mixed = tp_sum(dot(attended, wso[...]), 0)
 
     copies[7].wait()
     copies[8].wait()
@@ -493,9 +500,8 @@
     for h in range(1, heads):
         context = jnp.where(head_of == h, mixed[h * BLOCK : (h + 1) * BLOCK, :], context)
     copies[9].wait()
-    cross_mixed = self_mixed + tp_sum(dot(context.astype(BF16), wco[...]), 1)
-
-    resid[...] = cross_mixed
+    cross_mixed = tp_sum(dot(context.astype(BF16), wco[...]), 1)
+
     last_normed = layer_norm(cross_mixed, gains[2:3, :])
     copies[10].wait()
     units = jnp.maximum(dot(last_normed, wup[...]), 0.0).astype(BF16)
@@ -518,16 +524,15 @@
         )
     for copy in sent:
         copy.start()
+    for k, (target, _) in enumerate(seq_partners):
+        query_copy(k, target, me).wait_send()
+        part_copy(k, target, me).wait_send()
     total = resid[:, pl.ds(pl.multiple_of(my_tp * local, 128), local)] + dsend[my_tp].astype(F32)
     for copy in sent:
         copy.wait()
     for k in range(n_tp - 1):
         total = total + drecv[k].astype(F32)
     out_ref[...] = total[0:own_rows, :].astype(BF16)
-
-    for k, (target, _) in enumerate(seq_partners):
-        query_copy(k, target, me).wait_send()
-        part_copy(k, target, me).wait_send()
 
 
 def solution(mesh):
@@ -607,8 +612,8 @@
             vmem((sorted_rows, 2 * local), BF16),
             vmem((all_rows, local), BF16),
             vmem((all_rows, local), BF16),
-            vmem((2, BLOCK, width), BF16),
-            vmem((2, n_tp - 1, BLOCK, width), BF16),
+            vmem((2, 2 * own_rows, width // 2), BF16),
+            vmem((2, n_tp - 1, 2 * own_rows, width // 2), BF16),
             vmem((n_tp, BLOCK, local), BF16),
             vmem((n_tp - 1, BLOCK, local), BF16),
             dma((12,)),
@@ -621,30 +626,17 @@
             dma((3, n_tp - 1)),
             dma((3, n_tp - 1)),
         ]
-        return pl.pallas_call(
+        result = pl.pallas_call(
             functools.partial(kernel, n_seq, n_tp),
             out_shape=jax.ShapeDtypeStruct((own_rows, local), BF16),
-            in_specs=[pl.BlockSpec(memory_space=pl.ANY)] * 13,
+            in_specs=[pl.BlockSpec(memory_space=pltpu.HBM)] * 13,
             out_specs=pl.BlockSpec(memory_space=pltpu.VMEM),
             scratch_shapes=scratch,
             compiler_params=pltpu.CompilerParams(
-                collective_id=0, has_side_effects=True, vmem_limit_bytes=60 << 20
+                collective_id=0, has_side_effects=True, vmem_limit_bytes=50 << 20
             ),
-        )(
-            hidden,
-            norm_gains,
-            w_qkv,
-            w_self_out,
-            w_cross_q,
-            w_cross_out,
-            w_up,
-            w_down,
-            kv_cache,
-            encoder_kv,
-            lens,
-            page_table,
-            groups,
-        )
+        )(*[pltpu.with_memory_space_constraint(x, pltpu.HBM) for x in (hidden, norm_gains, w_qkv, w_self_out, w_cross_q, w_cross_out, w_up, w_down, kv_cache, encoder_kv, lens, page_table, groups)])
+        return result
 
     in_specs = (
         P("seq", None),

time: 43.5 us -> 41.3 us (0.949)
  Pallas kernels: 42.1 us -> 40.6 us
  local copies, waits for them, and re-layouts: 1.3 us -> 0.6 us
    pallas_call x1, Pallas kernels: 42.1 us -> 40.6 us  [per_device(): pl.pallas_call(functools.partial(kernel, n_seq, n_tp), out_shape=jax.Shap...]
    unnamed x1, local copies, waits for them, and re-layouts: 1.3 us -> 0.6 us
where the time goes in v3:
time: 41.3 us; the launch traced here: 41.2 us
  Pallas kernels  40.6 us (98%)
  local copies, waits for them, and re-layouts  0.6 us (1%)
    pallas_call x1, Pallas kernels, per_device(): pl.pallas_call(functools.partial(kernel, n_seq, n_tp), out_shape=jax.Shap...  40.6 us

profile of v3, /device:TPU:0, one launch (start us, length us, event | category | flops | bytes accessed | tf_op | source)
XLA Modules:
  0.0 41.2 jit_solution(10479862892788423765)
XLA Ops:
  0.0 40.6 %shard_map.127 = bf16[12,256]{1,0:T(8,128)(2,1)S(1)} custom-call(bf16[12,1024]{1,0:T(8,128)(2,1)} %hidden_h.1, f32[3,1024]{1,0:T(4,128)} %gains_h.1, bf16[3,1024,256]{2,1,0:T(8,128)(2,1)} %wqkv_h.1, bf16[256,1024]{1,0:T(8,128)(2,1)} %wso_h.1, bf16[1024,256]{1,0:T(8,128)(2,1)} %wcq_h.1, bf16[256,1024]{1,0:T(8,128)(2,1)} %wco_h.1, bf16[1024,2048]{1,0:T(8,128)(2,1)} %wup_h.1, ...), custom_call_target="tpu_custom_call" | custom-call | tf_op jit(solution)/shard_map/pallas_call | solution.py:629
  40.6 0.6 %copy.15 = bf16[12,256]{1,0:T(8,128)(2,1)} copy(bf16[12,256]{1,0:T(8,128)(2,1)S(1)} %shard_map.127) | data formatting | bytes 12288
